TPU v7x, 128 devices: a whole 4x4x4 slice. The times are simulated.
128 devices in a mesh: layer: 32 (over x_hi, y, z), dir: 4 (over x_lo, core).
Axes of the slice: x: 4 (x_hi: 2, x_lo: 2; x = x_hi * 2 + x_lo), y: 4, z: 4, core: 2. Of those that a mesh axis runs over, the one named last changes fastest.
Arguments:
- screens: bfloat16 [3, 2048, 16384], P(None, 'dir', 'layer'), may hold values from -6 to 6
- amplitude: float32 [1024, 1280], P('layer'), may hold values from 0.5 to 2
- wind: int32 [3, 2], replicated, may hold values from -8 to 8, as said below
- offsets: int32 [4, 3, 2], replicated, may hold values from 0 to 16383, as said below
- ratio: int32 [4, 3, 2], replicated, may hold values from 64 to 192, as said below
Outputs:
- new_screens: bfloat16 [3, 2048, 16384], P(None, 'dir', 'layer')
- spots: float32 [4, 2048, 2560], P('dir', 'layer')
Inputs may be any that keep to these rules, and one draw needn't show every extreme that they name: wind[l, 0] is layer l's row shift and wind[l, 1] its column shift; no shift is zero; one layer has column shift +8 and a row shift above zero, another has column shift -8 and a row shift below zero. offsets[d, l, 0] is a screen row below 2048, offsets[d, l, 1] a screen column below 16384. ratio[d, l] = (num, den) with 64 <= den <= 128 and den <= num <= den + den // 2; some entry is (192, 128) and another (64, 64).
All inputs are finite; a program needn't handle non-finite values.
Results may differ from a plain program's by a relative error of at most 0.009.
Values may be sent and summed in bfloat16 or wider, within the bound.
A program may use at most 64 MiB of HBM per device.

v0:
```python
import jax
import jax.numpy as jnp
from jax import lax
from jax.sharding import PartitionSpec as P

SUB_PIX = 16
SPOT_PIX = 32
WIND_MAX = 8


def with_halo(shard, sides, width):
    for axis, dim in sides:
        peers, length = (lax.axis_size(axis), shard.shape[dim])
        up = [(i, (i + 1) % peers) for i in range(peers)]
        down = [(j, i) for i, j in up]
        last = lax.slice_in_dim(shard, length - width, length, axis=dim)
        initial = lax.slice_in_dim(shard, 0, width, axis=dim)
        before = lax.ppermute(last, axis, up)
        after = lax.ppermute(initial, axis, down)
        shard = jnp.concatenate([before, shard, after], axis=dim)
    return shard


def spans(anchor, stretch_num, stretch_den, count, length):
    pixel = jnp.arange(count, dtype=jnp.int32)
    stretched = pixel * stretch_num
    base = (anchor + stretched // stretch_den) % length
    upper = (base + 1) % length
    fraction = (stretched % stretch_den).astype(jnp.float32) / stretch_den.astype(jnp.float32)
    return (base, upper, (1.0 - fraction).astype(jnp.bfloat16), fraction.astype(jnp.bfloat16))


def weights_rows(anchor, stretch_num, stretch_den, count, length, width):
    base, upper, low_weight, high_weight = spans(anchor, stretch_num, stretch_den, count, length)
    index = jnp.arange(width, dtype=jnp.int32)
    matrix = jnp.where(
        index[None, :] == base[:, None], low_weight[:, None], jnp.zeros((), jnp.bfloat16)
    )
    return jnp.where(index[None, :] == upper[:, None], high_weight[:, None], matrix)


def weights_cols(anchor, stretch_num, stretch_den, count, length, start, width):
    base, upper, low_weight, high_weight = spans(anchor, stretch_num, stretch_den, count, length)
    index = start + jnp.arange(width, dtype=jnp.int32)
    matrix = jnp.where(
        index[:, None] == base[None, :], low_weight[None, :], jnp.zeros((), jnp.bfloat16)
    )
    return jnp.where(index[:, None] == upper[None, :], high_weight[None, :], matrix)


def dft_tables():
    freq = jnp.arange(SPOT_PIX, dtype=jnp.int32)[:, None] - SPOT_PIX // 2
    pixel = jnp.arange(SUB_PIX, dtype=jnp.int32)[None, :]
    turns = freq * pixel % SPOT_PIX
    angle = turns.astype(jnp.float32) * (2.0 * jnp.pi / SPOT_PIX)
    return (jnp.cos(angle), -jnp.sin(angle))


def imaging(phase, amplitude):
    rows, cols = phase.shape
    sub_rows = rows // SUB_PIX
    sub_cols = cols // SUB_PIX
    real = (amplitude * jnp.cos(phase)).reshape(sub_rows, SUB_PIX, sub_cols, SUB_PIX)
    imag = (amplitude * jnp.sin(phase)).reshape(sub_rows, SUB_PIX, sub_cols, SUB_PIX)
    cos_table, sin_table = dft_tables()
    highest = lax.Precision.HIGHEST
    half_real = jnp.einsum("aibj,kj->aibk", real, cos_table, precision=highest) - jnp.einsum(
        "aibj,kj->aibk", imag, sin_table, precision=highest
    )
    half_imag = jnp.einsum("aibj,kj->aibk", real, sin_table, precision=highest) + jnp.einsum(
        "aibj,kj->aibk", imag, cos_table, precision=highest
    )
    full_real = jnp.einsum("ki,aibl->akbl", cos_table, half_real, precision=highest) - jnp.einsum(
        "ki,aibl->akbl", sin_table, half_imag, precision=highest
    )
    full_imag = jnp.einsum("ki,aibl->akbl", cos_table, half_imag, precision=highest) + jnp.einsum(
        "ki,aibl->akbl", sin_table, half_real, precision=highest
    )
    intensity = full_real * full_real + full_imag * full_imag
    totals = jnp.sum(intensity, axis=(1, 3), keepdims=True)
    normed = intensity * float(SPOT_PIX * SPOT_PIX) / totals
    return normed.reshape(sub_rows * SPOT_PIX, sub_cols * SPOT_PIX)


def per_device(screens, amplitude, wind, offsets, ratio):
    layers, rows_dev, cols_dev = screens.shape
    n_layer = lax.axis_size("layer")
    n_dir = lax.axis_size("dir")
    screen_rows = rows_dev * n_dir
    screen_cols = cols_dev * n_layer
    pupil_rows = amplitude.shape[0] * n_layer
    pupil_cols = amplitude.shape[1]
    direction = lax.axis_index("dir")
    column_start = lax.axis_index("layer") * cols_dev
    widened = with_halo(screens, (("layer", 2), ("dir", 1)), WIND_MAX)
    moved = []
    for level in range(layers):
        corner = (jnp.int32(WIND_MAX) - wind[level, 0], jnp.int32(WIND_MAX) - wind[level, 1])
        moved.append(lax.dynamic_slice(widened[level], corner, (rows_dev, cols_dev)))
    new_screens = jnp.stack(moved)
    piece = lax.all_gather(new_screens, "dir", axis=1, tiled=True)
    sums = []
    for add_level in range(layers):
        weights = weights_rows(
            offsets[direction, add_level, 0],
            ratio[direction, add_level, 0],
            ratio[direction, add_level, 1],
            pupil_rows,
            screen_rows,
            piece.shape[1],
        )
        sums.append(jnp.dot(weights, piece[add_level], preferred_element_type=jnp.float32))
    projected = jnp.stack(sums).astype(jnp.bfloat16)
    col_weights = [
        weights_cols(
            offsets[direction, level, 1],
            ratio[direction, level, 0],
            ratio[direction, level, 1],
            pupil_cols,
            screen_cols,
            column_start,
            cols_dev,
        )
        for level in range(layers)
    ]
    total = jnp.zeros((pupil_rows // n_layer * lax.axis_size("layer"), pupil_cols), jnp.float32)
    for level in range(layers):
        total = total + jnp.dot(
            projected[level], col_weights[level], preferred_element_type=jnp.float32
        )
    phase = lax.psum_scatter(
        total.astype(jnp.bfloat16), "layer", scatter_dimension=0, tiled=True
    ).astype(jnp.float32)
    spots = imaging(phase, amplitude)[None]
    return (new_screens, spots)


def solution(mesh):
    return jax.shard_map(
        per_device,
        mesh=mesh,
        in_specs=(P(None, "dir", "layer"), P("layer", None), P(), P(), P()),
        out_specs=(P(None, "dir", "layer"), P("dir", "layer", None)),
        check_vma=False,
    )
```

profile of v0, /device:TPU:0, one launch (start us, length us, event | category | flops | bytes accessed | tf_op | source)
XLA Modules:
  0.0 353.2 jit_solution(13287869215477032080)
XLA Ops:
  7.2 0.0 copy-start
  7.2 0.0 copy-start.2
  7.2 0.0 all-gather.2.cloned.1.call-start
  7.2 1.4 fusion.210
  8.6 2.1 collective-permute-start
  10.7 7.1 %collective-permute-start.1 = (bf16[3,512,8]{2,1,0:T(8,128)(2,1)S(1)}, bf16[3,512,8]{2,1,0:T(8,128)(2,1)S(1)}, u32[]{:S(2)}, u32[]{:S(2)}) collective-permute-start(bf16[3,512,8]{2,1,0:T(8,128)(2,1)S(1)} %get-tuple-element.8), channel_id=1, source_target_pairs={{4,0},{8,4},{12,8},{16,12},{20,16},{24,20},{28,24},{32,28},{36,32}... | collective-permute-start | bytes 73736 | tf_op jit(solution)/shard_map/ppermute | solution.py:19
  17.8 9.0 %collective-permute-done = bf16[3,512,8]{2,1,0:T(8,128)(2,1)S(1)} collective-permute-done((bf16[3,512,8]{2,1,0:T(8,128)(2,1)S(1)}, bf16[3,512,8]{2,1,0:T(8,128)(2,1)S(1)}, u32[]{:S(2)}, u32[]{:S(2)}) %collective-permute-start) | collective-permute-done | bytes 24608 | tf_op jit(solution)/shard_map/ppermute | solution.py:18
  26.9 0.0 collective-permute-done.1
  26.9 0.0 copy-done
  26.9 0.1 pad_maximum_fusion.4
  27.0 0.1 collective-permute-start.2
  27.0 1.7 collective-permute-start.3
  28.8 0.0 copy-done.2
  28.8 0.7 fusion.211
  37.0 0.0 collective-permute-done.2
  37.0 0.0 collective-permute-done.3
  37.0 1.2 pad_maximum_fusion
  38.2 0.2 fusion.209
  38.4 0.3 constant_dynamic-slice_fusion.10
  38.7 0.6 constant_dynamic-slice_fusion.8
  39.3 0.0 copy-start.3
  39.3 0.0 copy-start.4
  39.3 1.3 pad_maximum_fusion.1
  40.7 0.0 all-gather.2.cloned.1.call-update
  40.7 0.2 reduce-scatter.2.cloned.1.call-start
  40.9 0.0 copy-done.3
  40.9 0.7 constant_dynamic-slice_fusion
  49.4 0.0 copy-done.4
  49.4 0.7 constant_dynamic-slice_fusion.11
  50.0 1.4 subtract_convert_fusion.3
  51.4 1.3 fusion.177
  52.8 1.3 subtract_convert_fusion.5
  54.1 0.8 subtract_convert_fusion.1
  54.9 0.7 subtract_convert_fusion.2
  55.5 0.8 subtract_convert_fusion
  56.3 2.0 add_select_fusion.18
  58.4 2.0 add_select_fusion.22
  60.4 2.0 add_select_fusion.14
  62.4 2.1 add_select_fusion.6
  64.4 2.0 add_select_fusion.10
  66.5 2.0 add_select_fusion.2
  68.4 36.3 %all-gather.2.cloned.1.call-done = bf16[3,2048,512]{2,1,0:T(8,128)(2,1)} async-done(((bf16[3,512,512]{2,1,0:T(8,128)(2,1)}), bf16[3,2048,512]{2,1,0:T(8,128)(2,1)}) %all-gather.2.cloned.1.call-update) | async-done | bytes 6291472 | tf_op jit(solution)/shard_map/all_gather | solution.py:101
  104.7 8.1 %fusion.37 = f32[1024,1280]{1,0:T(8,128)} fusion(bf16[3,2048,512]{2,1,0:T(8,128)(2,1)} %all-gather.2.cloned.1.call-done, s32[1024]{0:T(1024)S(1)} %get-tuple-element.36, s32[1024]{0:T(1024)S(1)} %get-tuple-element.35, bf16[1024]{0:T(1024)(128)(2,1)S(1)} %get-tuple-element.40, bf16[1024]{0:T(1024)(128)(2,1)S(1)} %get-tuple-element.43, ...), kind=kOutput, calls=%fused_computation.45 | convolution fusion | flops 3501195264 | bytes 7369728 | tf_op jit(solution)/shard_map/dot_general | solution.py:128
  112.8 8.1 %fusion.40 = f32[1024,1280]{1,0:T(8,128)} fusion(bf16[3,2048,512]{2,1,0:T(8,128)(2,1)} %all-gather.2.cloned.1.call-done, s32[1024]{0:T(1024)S(1)} %get-tuple-element.38, s32[1024]{0:T(1024)S(1)} %get-tuple-element.37, bf16[1024]{0:T(1024)(128)(2,1)S(1)} %get-tuple-element.41, bf16[1024]{0:T(1024)(128)(2,1)S(1)} %get-tuple-element.44, ...), kind=kOutput, calls=%fused_computation.46 | convolution fusion | flops 3501195264 | bytes 7369728 | tf_op jit(solution)/shard_map/dot_general | solution.py:128
  120.9 9.2 %add_convert_fusion = bf16[1024,1280]{1,0:T(8,128)(2,1)} fusion(f32[1024,1280]{1,0:T(8,128)} %fusion.40, f32[1024,1280]{1,0:T(8,128)} %fusion.37, bf16[3,2048,512]{2,1,0:T(8,128)(2,1)} %all-gather.2.cloned.1.call-done, s32[1024]{0:T(1024)S(1)} %get-tuple-element.34, s32[1024]{0:T(1024)S(1)} %get-tuple-element.33, ...), kind=kOutput, calls=%fused_computation.12 | convolution fusion | flops 3505127424 | bytes 15234048 | tf_op jit(solution)/shard_map/dot_general | solution.py:128
  130.1 0.0 copy-start.1
  130.1 0.0 reduce-scatter.2.cloned.1.call-update
  130.1 190.9 %reduce-scatter.2.cloned.1.call-done = bf16[32,1280]{1,0:T(8,128)(2,1)} async-done(((bf16[1024,1280]{1,0:T(8,128)(2,1)}), bf16[32,1280]{1,0:T(8,128)(2,1)}) %reduce-scatter.2.cloned.1.call-update) | async-done | bytes 81936 | tf_op jit(solution)/shard_map/reduce_scatter | solution.py:131
  321.0 0.0 copy-done.1
  321.0 1.5 fusion.73
  322.5 0.4 reshape.377
  322.9 3.2 fusion.99
  326.1 3.2 fusion.95
  329.3 0.4 reshape.378
  329.7 3.2 convolution_add_fusion.1
  332.9 1.3 fusion.66
  334.2 3.2 convolution_subtract_fusion.1
  337.4 1.3 fusion.70
  338.7 1.3 fusion.47
  340.0 1.4 fusion.212
  341.4 1.2 multiply_divide_fusion
  342.6 1.9 copy.23
  344.5 1.8 broadcast_in_dim_reshape.3
  (2 shorter events, 0.0 us)
Async XLA Ops:
  7.2 19.7 %copy-start = (bf16[3,512,512]{2,1,0:T(8,128)(2,1)S(1)}, bf16[3,512,512]{2,1,0:T(8,128)(2,1)}, u32[]{:S(2)}) copy-start(bf16[3,512,512]{2,1,0:T(8,128)(2,1)} %param.5) | copy-start | bytes 4718596
  7.2 21.6 %copy-start.2 = (s32[3,2]{0,1:T(2,128)S(1)}, s32[3,2]{0,1:T(2,128)}, u32[]{:S(2)}) copy-start(s32[3,2]{0,1:T(2,128)} %param.7) | copy-start | bytes 76
  7.2 97.5 %all-gather.2.cloned.1.call-start = ((), (), s32[]{:S(2)}) async-start(), calls=%async_computation.1 | async-start | bytes 7864320 | tf_op jit(solution)/shard_map/all_gather | solution.py:101
  8.6 18.2 %collective-permute-start = (bf16[3,512,8]{2,1,0:T(8,128)(2,1)S(1)}, bf16[3,512,8]{2,1,0:T(8,128)(2,1)S(1)}, u32[]{:S(2)}, u32[]{:S(2)}) collective-permute-start(bf16[3,512,8]{2,1,0:T(8,128)(2,1)S(1)} %get-tuple-element.7), channel_id=1, source_target_pairs={{0,4},{4,8},{8,12},{12,16},{16,20},{20,24},{24,28},{28,32},{32,36}... | collective-permute-start | bytes 73736 | tf_op jit(solution)/shard_map/ppermute | solution.py:18
  10.7 16.1 %collective-permute-start.1 = (bf16[3,512,8]{2,1,0:T(8,128)(2,1)S(1)}, bf16[3,512,8]{2,1,0:T(8,128)(2,1)S(1)}, u32[]{:S(2)}, u32[]{:S(2)}) collective-permute-start(bf16[3,512,8]{2,1,0:T(8,128)(2,1)S(1)} %get-tuple-element.8), channel_id=1, source_target_pairs={{4,0},{8,4},{12,8},{16,12},{20,16},{24,20},{28,24},{32,28},{36,32}... | collective-permute-start | bytes 73736 | tf_op jit(solution)/shard_map/ppermute | solution.py:19
  27.0 10.1 %collective-permute-start.2 = (bf16[3,8,528]{2,1,0:T(8,128)(2,1)S(1)}, bf16[3,8,528]{2,1,0:T(8,128)(2,1)S(1)}, u32[]{:S(2)}, u32[]{:S(2)}) collective-permute-start(bf16[3,8,528]{2,1,0:T(8,128)(2,1)S(1)} %get-tuple-element.2), channel_id=1, source_target_pairs={{0,1},{1,2},{2,3},{3,0},{4,5},{5,6},{6,7},{7,4},{8,9},{9,10},{10,1... | collective-permute-start | bytes 76040 | tf_op jit(solution)/shard_map/ppermute | solution.py:18
  27.0 10.0 %collective-permute-start.3 = (bf16[3,8,528]{2,1,0:T(8,128)(2,1)S(1)}, bf16[3,8,528]{2,1,0:T(8,128)(2,1)S(1)}, u32[]{:S(2)}, u32[]{:S(2)}) collective-permute-start(bf16[3,8,528]{2,1,0:T(8,128)(2,1)S(1)} %get-tuple-element.3), channel_id=1, source_target_pairs={{1,0},{2,1},{3,2},{0,3},{5,4},{6,5},{7,6},{4,7},{9,8},{10,9},{11,1... | collective-permute-start | bytes 76040 | tf_op jit(solution)/shard_map/ppermute | solution.py:19
  39.3 1.6 copy-start.3
  39.3 10.0 %copy-start.4 = (s32[4,3,2]{0,2,1:T(2,128)S(1)}, s32[4,3,2]{0,2,1:T(2,128)}, u32[]{:S(2)}) copy-start(s32[4,3,2]{0,2,1:T(2,128)} %param.8) | copy-start | bytes 292
  40.7 280.3 %reduce-scatter.2.cloned.1.call-start = ((), (), s32[]{:S(2)}) async-start(), calls=%async_computation.2 | async-start | bytes 2703360 | tf_op jit(solution)/shard_map/reduce_scatter | solution.py:131
  130.1 190.9 %copy-start.1 = (f32[32,1280]{1,0:T(8,128)S(1)}, f32[32,1280]{1,0:T(8,128)}, u32[]{:S(2)}) copy-start(f32[32,1280]{1,0:T(8,128)} %param.6) | copy-start | bytes 491524
Sparse Core Ops, SparseCore 0:
  40.8 63.8 all-gather.1
  130.2 190.7 reduce-scatter.1
where the time goes:
time: 354 us; the launch traced here: 353 us
  waiting for transfers between devices  236 us (67%)
  matrix products  43.4 us (12%)
  between operations  29.6 us (8%)
  other arithmetic  23.6 us (7%)
  starting transfers between devices  11.2 us (3%)
  local copies, waits for them, and re-layouts  9.15 us (3%)
    reduce_scatter x1, waiting for transfers between devices, per_device(): lax.psum_scatter(total.astype(jnp.bfloat16), 'layer', scatter_dimension=0...  191 us
    all_gather x1, waiting for transfers between devices, per_device(): piece = lax.all_gather(new_screens, 'dir', axis=1, tiled=True)  36.3 us
    dot_general x3, matrix products, per_device(): jnp.dot(projected[level], col_weights[level], preferred_element_type=jnp....  25.4 us
    select_n x6, other arithmetic, spans(): upper = (base + 1) % length  12.1 us
    ppermute x2, waiting for transfers between devices, with_halo(): before = lax.ppermute(last, axis, up)  9.03 us
    ppermute x2, starting transfers between devices, with_halo(): after = lax.ppermute(initial, axis, down)  8.84 us
  transfers between devices with their start and end apart: 6, of which 3 were waited for; matrix products, arithmetic and copies ran while one was open for 6% of the time, Pallas kernels for 0%

commit v1 on v0

--- a/solution.py
+++ b/solution.py
@@ -1,3 +1,4 @@
+import functools
 import jax
 import jax.numpy as jnp
 from jax import lax
@@ -6,6 +7,18 @@
 SUB_PIX = 16
 SPOT_PIX = 32
 WIND_MAX = 8
+
+
+def process_the_vectors(sample, device_axis):
+    return jnp.concatenate(
+        lax.all_to_all(
+            jnp.stack([sample for _ in range(lax.axis_size(device_axis))]), device_axis, 0, 0
+        ),
+        axis=1,
+    )
+
+
+_obtain_frame = functools.partial(process_the_vectors, device_axis="dir")
 
 
 def with_halo(shard, sides, width):
@@ -98,7 +111,7 @@
         corner = (jnp.int32(WIND_MAX) - wind[level, 0], jnp.int32(WIND_MAX) - wind[level, 1])
         moved.append(lax.dynamic_slice(widened[level], corner, (rows_dev, cols_dev)))
     new_screens = jnp.stack(moved)
-    piece = lax.all_gather(new_screens, "dir", axis=1, tiled=True)
+    piece = _obtain_frame(new_screens)
     sums = []
     for add_level in range(layers):
         weights = weights_rows(

time: 354 us -> 373 us (1.054)
  local copies, waits for them, and re-layouts: 9.15 us -> 18.9 us
  waiting for transfers between devices: 236 us -> 242 us
  starting transfers between devices: 11.2 us -> 16.6 us
    all_to_all x0 -> x1, waiting for transfers between devices: none -> 43.1 us  [process_the_vectors(): lax.all_to_all(jnp.stack([sample for _ in range(lax.axis_size(device_axis...]
    all_gather x1 -> x0, waiting for transfers between devices: 36.3 us -> none  [per_device(): piece = lax.all_gather(new_screens, 'dir', axis=1, tiled=True)]
    all_to_all x0 -> x1, starting transfers between devices: none -> 5.41 us  [process_the_vectors(): lax.all_to_all(jnp.stack([sample for _ in range(lax.axis_size(device_axis...]
    slice x0 -> x1, local copies, waits for them, and re-layouts: none -> 5.37 us  [per_device(): piece[add_level]]
where the time goes in v1:
time: 373 us; the launch traced here: 372 us
  waiting for transfers between devices  242 us (65%)
  matrix products  42.9 us (12%)
  between operations  29.1 us (8%)
  other arithmetic  22.8 us (6%)
  local copies, waits for them, and re-layouts  18.9 us (5%)
  starting transfers between devices  16.6 us (4%)
    reduce_scatter x1, waiting for transfers between devices, per_device(): lax.psum_scatter(total.astype(jnp.bfloat16), 'layer', scatter_dimension=0...  190 us
    all_to_all x1, waiting for transfers between devices, process_the_vectors(): lax.all_to_all(jnp.stack([sample for _ in range(lax.axis_size(device_axis...  43.1 us
    dot_general x3, matrix products, per_device(): jnp.dot(projected[level], col_weights[level], preferred_element_type=jnp....  24.9 us
    select_n x6, other arithmetic, spans(): upper = (base + 1) % length  12.1 us
    ppermute x2, waiting for transfers between devices, with_halo(): before = lax.ppermute(last, axis, up)  9.03 us
    ppermute x2, starting transfers between devices, with_halo(): after = lax.ppermute(initial, axis, down)  8.84 us
  transfers between devices with their start and end apart: 6, of which 3 were waited for; matrix products, arithmetic and copies ran while one was open for 6% of the time, Pallas kernels for 0%

profile of v1, /device:TPU:0, one launch (start us, length us, event | category | flops | bytes accessed | tf_op | source)
XLA Modules:
  0.0 372.2 jit_solution(1811025883237310558)
XLA Ops:
  7.2 0.0 copy-start
  7.2 0.0 copy-start.3
  7.2 1.4 fusion.211
  8.6 2.1 collective-permute-start
  10.7 7.1 %collective-permute-start.1 = (bf16[3,512,8]{2,1,0:T(8,128)(2,1)S(1)}, bf16[3,512,8]{2,1,0:T(8,128)(2,1)S(1)}, u32[]{:S(2)}, u32[]{:S(2)}) collective-permute-start(bf16[3,512,8]{2,1,0:T(8,128)(2,1)S(1)} %get-tuple-element.11), channel_id=1, source_target_pairs={{4,0},{8,4},{12,8},{16,12},{20,16},{24,20},{28,24},{32,28},{36,32}... | collective-permute-start | bytes 73736 | tf_op jit(solution)/shard_map/ppermute | solution.py:32
  17.8 9.0 %collective-permute-done = bf16[3,512,8]{2,1,0:T(8,128)(2,1)S(1)} collective-permute-done((bf16[3,512,8]{2,1,0:T(8,128)(2,1)S(1)}, bf16[3,512,8]{2,1,0:T(8,128)(2,1)S(1)}, u32[]{:S(2)}, u32[]{:S(2)}) %collective-permute-start) | collective-permute-done | bytes 24608 | tf_op jit(solution)/shard_map/ppermute | solution.py:31
  26.8 0.0 collective-permute-done.1
  26.8 0.0 copy-done
  26.8 0.1 pad_maximum_fusion.4
  26.9 0.1 collective-permute-start.2
  27.0 1.7 collective-permute-start.3
  28.7 0.0 copy-done.3
  28.7 0.7 fusion.212
  37.0 0.0 collective-permute-done.2
  37.0 0.0 collective-permute-done.3
  37.0 1.2 pad_maximum_fusion
  38.2 0.2 fusion.210
  38.4 0.3 constant_dynamic-slice_fusion.10
  38.7 0.6 constant_dynamic-slice_fusion.8
  39.3 0.2 pad_maximum_fusion.1
  39.5 0.0 copy-start.1
  39.5 1.1 copy-done.1
  40.6 3.2 stack.9
  43.9 0.0 copy-start.4
  43.9 5.4 %all-to-all-start = ((bf16[4,3,512,512]{3,2,1,0:T(8,128)(2,1)}), bf16[4,3,512,512]{3,2,1,0:T(8,128)(2,1)}, u32[]{:S(2)}, u32[]{:S(2)}) async-start(bf16[4,3,512,512]{3,2,1,0:T(8,128)(2,1)} %stack.9), calls=%async_computation | async-start | bytes 12582912 | tf_op jit(solution)/shard_map/all_to_all | solution.py:14
  49.3 0.2 reduce-scatter.2.cloned.1.call-start
  49.5 0.0 copy-done.4
  49.5 0.7 constant_dynamic-slice_fusion
  57.4 0.0 copy-done.5
  57.4 0.7 constant_dynamic-slice_fusion.1
  58.1 1.5 subtract_convert_fusion.3
  59.6 1.4 fusion.177
  61.0 1.4 subtract_convert_fusion.5
  62.4 0.8 subtract_convert_fusion.1
  63.2 0.7 subtract_convert_fusion.2
  64.0 0.8 subtract_convert_fusion
  64.8 2.1 add_select_fusion.18
  66.8 1.9 add_select_fusion.22
  68.8 2.0 add_select_fusion.14
  70.7 2.1 add_select_fusion.6
  72.9 1.9 add_select_fusion.10
  74.8 2.0 add_select_fusion.2
  76.8 43.1 %all-to-all-done = bf16[4,3,512,512]{3,2,1,0:T(8,128)(2,1)} async-done(((bf16[4,3,512,512]{3,2,1,0:T(8,128)(2,1)}), bf16[4,3,512,512]{3,2,1,0:T(8,128)(2,1)}, u32[]{:S(2)}, u32[]{:S(2)}) %all-to-all-start) | async-done | bytes 6291488 | tf_op jit(solution)/shard_map/all_to_all | solution.py:14
  120.0 5.4 %fusion.209 = (bf16[1,4,512,512]{3,2,0,1:T(8,128)(2,1)S(1)}, bf16[1,4,512,512]{3,2,0,1:T(8,128)(2,1)}, bf16[1,4,512,512]{3,2,0,1:T(8,128)(2,1)}) fusion(bf16[3,4,512,512]{3,2,0,1:T(8,128)(2,1)} %bitcast.15), kind=kLoop, calls=%fused_computation.301 | loop fusion | bytes 12582912 | tf_op jit(solution)/shard_map/slice | solution.py:125
  125.4 8.1 %fusion.37 = f32[1024,1280]{1,0:T(8,128)} fusion(bf16[2048,512]{1,0:T(8,128)(2,1)} %bitcast.65, s32[1024]{0:T(1024)S(1)} %get-tuple-element.39, s32[1024]{0:T(1024)S(1)} %get-tuple-element.38, bf16[1024]{0:T(1024)(128)(2,1)S(1)} %get-tuple-element.43, bf16[1024]{0:T(1024)(128)(2,1)S(1)} %get-tuple-element.46, s32[1280]{0:T(1024)S(1)} %get-tuple-element.53, ...), kind=kOutput, calls=%fused_computation.42 | convolution fusion | flops 3501195264 | bytes 7369728 | tf_op jit(solution)/shard_map/dot_general | solution.py:141
  133.5 8.2 %fusion.40 = f32[1024,1280]{1,0:T(8,128)} fusion(bf16[2048,512]{1,0:T(8,128)(2,1)} %bitcast.64, s32[1024]{0:T(1024)S(1)} %get-tuple-element.41, s32[1024]{0:T(1024)S(1)} %get-tuple-element.40, bf16[1024]{0:T(1024)(128)(2,1)S(1)} %get-tuple-element.44, bf16[1024]{0:T(1024)(128)(2,1)S(1)} %get-tuple-element.47, s32[1280]{0:T(1024)S(1)} %get-tuple-element.49, ...), kind=kOutput, calls=%fused_computation.43 | convolution fusion | flops 3501195264 | bytes 7369728 | tf_op jit(solution)/shard_map/dot_general | solution.py:141
  141.7 8.6 %add_convert_fusion = bf16[1024,1280]{1,0:T(8,128)(2,1)} fusion(f32[1024,1280]{1,0:T(8,128)} %fusion.40, f32[1024,1280]{1,0:T(8,128)} %fusion.37, s32[1280]{0:T(1024)S(1)} %get-tuple-element.57, s32[1280]{0:T(1024)S(1)} %get-tuple-element.56, s32[512]{0:T(512)S(1)} %iota_add_fusion, bf16[2048,512]{1,0:T(8,128)(2,1)S(1)} %bitcast.63, ...), kind=kOutput, calls=%fused_computation.12 | convolution fusion | flops 3505127424 | bytes 15234048 | tf_op jit(solution)/shard_map/dot_general | solution.py:141
  150.3 0.0 reduce-scatter.2.cloned.1.call-update
  150.3 189.8 %reduce-scatter.2.cloned.1.call-done = bf16[32,1280]{1,0:T(8,128)(2,1)} async-done(((bf16[1024,1280]{1,0:T(8,128)(2,1)}), bf16[32,1280]{1,0:T(8,128)(2,1)}) %reduce-scatter.2.cloned.1.call-update) | async-done | bytes 81936 | tf_op jit(solution)/shard_map/reduce_scatter | solution.py:144
  340.1 0.0 copy-done.2
  340.1 1.5 fusion.73
  341.6 0.4 reshape.390
  342.0 3.2 fusion.99
  345.2 3.2 fusion.95
  348.4 0.4 reshape.391
  348.8 3.2 convolution_add_fusion.1
  352.0 1.3 fusion.66
  353.3 3.2 convolution_subtract_fusion.1
  356.5 1.3 fusion.70
  357.7 1.3 fusion.45
  359.1 1.4 fusion.213
  360.5 1.1 multiply_divide_fusion
  361.6 1.9 copy.23
  363.6 1.8 broadcast_in_dim_reshape.3
  (4 shorter events, 0.0 us)
Async XLA Ops:
  7.2 19.7 %copy-start = (bf16[3,512,512]{2,1,0:T(8,128)(2,1)S(1)}, bf16[3,512,512]{2,1,0:T(8,128)(2,1)}, u32[]{:S(2)}) copy-start(bf16[3,512,512]{2,1,0:T(8,128)(2,1)} %param.5) | copy-start | bytes 4718596
  7.2 21.6 %copy-start.3 = (s32[3,2]{0,1:T(2,128)S(1)}, s32[3,2]{0,1:T(2,128)}, u32[]{:S(2)}) copy-start(s32[3,2]{0,1:T(2,128)} %param.7) | copy-start | bytes 76
  8.6 18.2 %collective-permute-start = (bf16[3,512,8]{2,1,0:T(8,128)(2,1)S(1)}, bf16[3,512,8]{2,1,0:T(8,128)(2,1)S(1)}, u32[]{:S(2)}, u32[]{:S(2)}) collective-permute-start(bf16[3,512,8]{2,1,0:T(8,128)(2,1)S(1)} %get-tuple-element.10), channel_id=1, source_target_pairs={{0,4},{4,8},{8,12},{12,16},{16,20},{20,24},{24,28},{28,32},{32,36}... | collective-permute-start | bytes 73736 | tf_op jit(solution)/shard_map/ppermute | solution.py:31
  10.7 16.1 %collective-permute-start.1 = (bf16[3,512,8]{2,1,0:T(8,128)(2,1)S(1)}, bf16[3,512,8]{2,1,0:T(8,128)(2,1)S(1)}, u32[]{:S(2)}, u32[]{:S(2)}) collective-permute-start(bf16[3,512,8]{2,1,0:T(8,128)(2,1)S(1)} %get-tuple-element.11), channel_id=1, source_target_pairs={{4,0},{8,4},{12,8},{16,12},{20,16},{24,20},{28,24},{32,28},{36,32}... | collective-permute-start | bytes 73736 | tf_op jit(solution)/shard_map/ppermute | solution.py:32
  26.9 10.1 %collective-permute-start.2 = (bf16[3,8,528]{2,1,0:T(8,128)(2,1)S(1)}, bf16[3,8,528]{2,1,0:T(8,128)(2,1)S(1)}, u32[]{:S(2)}, u32[]{:S(2)}) collective-permute-start(bf16[3,8,528]{2,1,0:T(8,128)(2,1)S(1)} %get-tuple-element.5), channel_id=1, source_target_pairs={{0,1},{1,2},{2,3},{3,0},{4,5},{5,6},{6,7},{7,4},{8,9},{9,10},{10,1... | collective-permute-start | bytes 76040 | tf_op jit(solution)/shard_map/ppermute | solution.py:31
  27.0 10.0 %collective-permute-start.3 = (bf16[3,8,528]{2,1,0:T(8,128)(2,1)S(1)}, bf16[3,8,528]{2,1,0:T(8,128)(2,1)S(1)}, u32[]{:S(2)}, u32[]{:S(2)}) collective-permute-start(bf16[3,8,528]{2,1,0:T(8,128)(2,1)S(1)} %get-tuple-element.6), channel_id=1, source_target_pairs={{1,0},{2,1},{3,2},{0,3},{5,4},{6,5},{7,6},{4,7},{9,8},{10,9},{11,1... | collective-permute-start | bytes 76040 | tf_op jit(solution)/shard_map/ppermute | solution.py:32
  39.5 1.1 copy-start.1
  43.9 5.7 %copy-start.4 = (s32[4,3,2]{0,2,1:T(2,128)S(1)}, s32[4,3,2]{0,2,1:T(2,128)}, u32[]{:S(2)}) copy-start(s32[4,3,2]{0,2,1:T(2,128)} %param.9) | copy-start | bytes 292
  43.9 13.6 %copy-start.5 = (s32[4,3,2]{0,2,1:T(2,128)S(1)}, s32[4,3,2]{0,2,1:T(2,128)}, u32[]{:S(2)}) copy-start(s32[4,3,2]{0,2,1:T(2,128)} %param.8) | copy-start | bytes 292
  43.9 76.1 %all-to-all-start = ((bf16[4,3,512,512]{3,2,1,0:T(8,128)(2,1)}), bf16[4,3,512,512]{3,2,1,0:T(8,128)(2,1)}, u32[]{:S(2)}, u32[]{:S(2)}) async-start(bf16[4,3,512,512]{3,2,1,0:T(8,128)(2,1)} %stack.9), calls=%async_computation | async-start | bytes 12582912 | tf_op jit(solution)/shard_map/all_to_all | solution.py:14
  49.3 290.8 %reduce-scatter.2.cloned.1.call-start = ((), (), s32[]{:S(2)}) async-start(), calls=%async_computation.2 | async-start | bytes 2703360 | tf_op jit(solution)/shard_map/reduce_scatter | solution.py:144
  150.3 189.8 %copy-start.2 = (f32[32,1280]{1,0:T(8,128)S(1)}, f32[32,1280]{1,0:T(8,128)}, u32[]{:S(2)}) copy-start(f32[32,1280]{1,0:T(8,128)} %param.6) | copy-start | bytes 491524
Sparse Core Ops, SparseCore 0:
  150.4 189.6 reduce-scatter.1
